TPU v7x, 32 devices: a whole 2x2x4 slice. The times are simulated.
32 devices in a mesh: rows: 8 (over z, y), ch: 4 (over x, core).
Axes of the slice: x: 2, y: 2, z: 4, core: 2. Of those that a mesh axis runs over, the one named last changes fastest.
Arguments:
- tile_image: bfloat16 [768, 256, 256], P('ch', 'rows'), may hold values from -23 to 23
- spectral_filter: float32 [2, 768, 256, 256], P(None, 'ch', 'rows'), may hold values from -4 to 4
- conv_taps: float32 [768, 9], P('ch'), may hold values from -4 to 4
- norm_gain: float32 [768], replicated, may hold values from 0.25 to 1.75
- up_weight: bfloat16 [768, 3072], P(None, 'ch'), may hold values from -0.21875 to 0.21875
- down_weight: bfloat16 [3072, 768], P('ch'), may hold values from -0.109375 to 0.109375
- upstream: bfloat16 [768, 256, 256], P('ch', 'rows'), may hold values from -5 to 5
Outputs:
- block_out: bfloat16 [768, 256, 256], P('ch', 'rows')
- grad_image: float32 [768, 256, 256], P('ch', 'rows')
- grad_filter: float32 [2, 768, 256, 256], P(None, 'ch', 'rows')
All inputs are finite; a program needn't handle non-finite values.
Results may differ from a plain program's by a relative error of at most 0.012.
Values may be sent and summed in bfloat16 or wider, within the bound.
A program may use at most 192 MiB of HBM per device.

v0:
```python
import math
import jax
import jax.numpy as jnp
from jax import lax
from jax.sharding import PartitionSpec as P

norm_epsilon = 1e-05
root_half = 0.7071067811865476
density = 0.3989422804014327


def with_halo(block, sides, width):
    for axis, dim in sides:
        count = lax.axis_size(axis)
        forward = [(i, i + 1) for i in range(count - 1)]
        backward = [(target, source) for source, target in forward]
        low = lax.ppermute(
            lax.slice_in_dim(block, block.shape[dim] - width, None, axis=dim), axis, forward
        )
        high = lax.ppermute(lax.slice_in_dim(block, 0, width, axis=dim), axis, backward)
        block = jnp.concatenate([low, block, high], axis=dim)
    return block


def contract(form, left, right):
    return jnp.einsum(
        form, left, right, precision=lax.Precision.HIGHEST, preferred_element_type=jnp.float32
    )


def angle_tables(length):
    indices = jnp.arange(length, dtype=jnp.int32)
    products = indices[:, None] * indices[None, :] % length
    angles = products.astype(jnp.float32) * (2.0 * math.pi / length)
    return (jnp.cos(angles), jnp.sin(angles))


def filter_pass(signal, kernel_re, kernel_im):
    col_len = signal.shape[2]
    cos_w, sin_w = angle_tables(col_len)
    head_re = contract("chw,kw->ckh", signal, cos_w)
    head_im = -contract("chw,kw->ckh", signal, sin_w)
    col_re, col_im = (
        lax.all_to_all(
            head_re.astype(jnp.bfloat16), "rows", split_axis=1, concat_axis=2, tiled=True
        ).astype(head_re.dtype),
        lax.all_to_all(
            head_im.astype(jnp.bfloat16), "rows", split_axis=1, concat_axis=2, tiled=True
        ).astype(head_im.dtype),
    )
    row_len = col_re.shape[2]
    cos_h, sin_h = angle_tables(row_len)
    spec_re = contract("cwh,kh->cwk", col_re, cos_h) + contract("cwh,kh->cwk", col_im, sin_h)
    spec_im = contract("cwh,kh->cwk", col_im, cos_h) - contract("cwh,kh->cwk", col_re, sin_h)
    prod_re = kernel_re * spec_re - kernel_im * spec_im
    prod_im = kernel_re * spec_im + kernel_im * spec_re
    back_re = contract("cwk,kh->cwh", prod_re, cos_h) - contract("cwk,kh->cwh", prod_im, sin_h)
    back_im = contract("cwk,kh->cwh", prod_im, cos_h) + contract("cwk,kh->cwh", prod_re, sin_h)
    row_re, row_im = (
        lax.all_to_all(
            back_re.astype(jnp.bfloat16), "rows", split_axis=2, concat_axis=1, tiled=True
        ).astype(back_re.dtype),
        lax.all_to_all(
            back_im.astype(jnp.bfloat16), "rows", split_axis=2, concat_axis=1, tiled=True
        ).astype(back_im.dtype),
    )
    outcome = contract("ckh,kw->chw", row_re, cos_w) - contract("ckh,kw->chw", row_im, sin_w)
    return (outcome * (1.0 / (row_len * col_len)), spec_re, spec_im)


def depthwise(signal, tap_weights):
    token_row_count, col_count = (signal.shape[1], signal.shape[2])
    padded = with_halo(signal.astype(jnp.bfloat16), (("rows", 1),), 1).astype(signal.dtype)
    padded = jnp.pad(padded, ((0, 0), (0, 0), (1, 1)))
    running = jnp.zeros_like(signal)
    for row_off in range(3):
        for col_off in range(3):
            running = (
                running
                + tap_weights[:, 3 * row_off + col_off][:, None, None]
                * padded[:, row_off : row_off + token_row_count, col_off : col_off + col_count]
            )
    return running


def layer_norm(whole):
    values = whole.astype(jnp.float32)
    centred = values - jnp.mean(values, axis=0)[None]
    inv_std = lax.rsqrt(jnp.mean(centred * centred, axis=0) + norm_epsilon)
    return (centred * inv_std[None], inv_std)


def gelu_slope(pre_act):
    return 0.5 * (1.0 + lax.erf(pre_act * root_half)) + pre_act * density * jnp.exp(
        -0.5 * pre_act * pre_act
    )


def norm_back(normed_gradient, normed, inv_std, gain):
    weighted = normed_gradient * gain[None, :, None, None]
    mean_one = jnp.mean(weighted, axis=1, keepdims=True)
    second = jnp.mean(weighted * normed[None], axis=1, keepdims=True)
    return inv_std[None, None] * (weighted - mean_one - normed[None] * second)


def settle(partials):
    return jnp.sum(
        lax.optimization_barrier(partials.astype(jnp.bfloat16)).astype(jnp.float32), axis=0
    )


def to_tokens(values):
    return lax.all_to_all(values, "ch", split_axis=2, concat_axis=0, tiled=True)


def to_channels(values):
    return lax.all_to_all(
        values.astype(jnp.bfloat16), "ch", split_axis=0, concat_axis=2, tiled=True
    ).astype(values.dtype)


def on_device(tile_image, spectral_filter, conv_taps, norm_gain, up_weight, down_weight, upstream):
    signal = tile_image.astype(jnp.float32)
    filtered, spec_re, spec_im = filter_pass(signal, spectral_filter[0], spectral_filter[1])
    hidden_state = signal + depthwise(filtered, conv_taps)
    rounded = hidden_state.astype(jnp.bfloat16)
    gain_column = norm_gain[:, None, None]
    full_up, full_down = (
        lax.all_gather(up_weight, "ch", axis=1, tiled=True),
        lax.all_gather(down_weight, "ch", axis=0, tiled=True),
    )
    blocks = lax.axis_size("ch")
    channels, hidden_units = (full_up.shape[0], full_up.shape[1])
    hidden_share_units = hidden_units // blocks
    normed, inv_std = layer_norm(to_tokens(rounded))
    scaled = (normed * gain_column).astype(jnp.bfloat16)
    pre_act = jnp.einsum("chw,cf->fhw", scaled, full_up, preferred_element_type=jnp.float32)
    activated = jax.nn.gelu(pre_act, approximate=False).astype(jnp.bfloat16)
    token_row_count, col_count = (activated.shape[1], activated.shape[2])
    partials = jnp.einsum(
        "bfhw,bfc->bchw",
        activated.reshape(blocks, hidden_share_units, token_row_count, col_count),
        full_down.reshape(blocks, hidden_share_units, channels),
        preferred_element_type=jnp.float32,
    )
    out_sum = to_channels(settle(partials))
    block_out = (hidden_state + out_sum).astype(jnp.bfloat16)
    whole_dy = to_tokens(upstream)
    grad_act = jnp.einsum("chw,fc->fhw", whole_dy, full_down, preferred_element_type=jnp.float32)
    preactivation_gradient = (grad_act * gelu_slope(pre_act)).astype(jnp.bfloat16)
    normed_gradient = jnp.einsum(
        "pjra,spj->psra",
        preactivation_gradient.reshape(blocks, hidden_share_units, token_row_count, col_count),
        full_up.reshape(channels, blocks, hidden_share_units),
        preferred_element_type=jnp.float32,
    )
    grad_mlp = to_channels(settle(norm_back(normed_gradient, normed, inv_std, norm_gain)))
    grad_hidden = upstream.astype(jnp.float32) + grad_mlp
    grad_filtered = depthwise(grad_hidden, conv_taps[:, ::-1])
    adjoint, grad_re, grad_im = filter_pass(grad_filtered, spectral_filter[0], -spectral_filter[1])
    grad_image = grad_hidden + adjoint
    factor = 1.0 / (tile_image.shape[2] * spec_re.shape[2])
    grad_filter = jnp.stack(
        [
            (grad_re * spec_re + grad_im * spec_im) * factor,
            (grad_im * spec_re - grad_re * spec_im) * factor,
        ]
    )
    return (block_out, grad_image, grad_filter)


def solution(mesh):
    return jax.shard_map(
        on_device,
        mesh=mesh,
        in_specs=(
            P("ch", "rows", None),
            P(None, "ch", "rows", None),
            P("ch", None),
            P(),
            P(None, "ch"),
            P("ch", None),
            P("ch", "rows", None),
        ),
        out_specs=(P("ch", "rows", None), P("ch", "rows", None), P(None, "ch", "rows", None)),
        check_vma=False,
    )
```

profile of v0, /device:TPU:0, one launch (start us, length us, event | category | flops | bytes accessed | tf_op | source)
XLA Modules:
  0.0 1455.8 jit_solution(15047290855060164912)
XLA Ops:
  7.2 10.0 fusion.76
  17.2 7.8 copy.221
  24.9 7.9 all-to-all-start.1
  32.8 8.2 convert_bitcast_fusion.3
  41.0 7.6 copy.217
  48.6 77.4 %all-to-all-done.1 = bf16[192,256,32]{0,2,1:T(8,128)(2,1)} async-done(((bf16[192,256,32]{0,2,1:T(8,128)(2,1)}), bf16[192,256,32]{0,2,1:T(8,128)(2,1)}, u32[]{:S(2)}, u32[]{:S(2)}) %all-to-all-start.1) | async-done | bytes 3145760 | tf_op jit(solution)/shard_map/all_to_all | solution.py:47
  148.3 75.1 %all-to-all-done = bf16[192,256,32]{0,2,1:T(8,128)(2,1)} async-done(((bf16[192,256,32]{0,2,1:T(8,128)(2,1)}), bf16[192,256,32]{0,2,1:T(8,128)(2,1)}, u32[]{:S(2)}, u32[]{:S(2)}) %all-to-all-start) | async-done | bytes 3145760 | tf_op jit(solution)/shard_map/all_to_all | solution.py:44
  235.3 8.3 fusion.125
  250.1 15.3 %fusion.64 = (f32[192,32,256]{2,1,0:T(8,128)}, f32[192,32,256]{2,1,0:T(8,128)}, f32[192,32,256]{2,1,0:T(8,128)}) fusion(f32[192,32,256]{2,1,0:T(8,128)} %convolution_subtract_fusion.1, f32[2,192,32,256]{3,2,1,0:T(8,128)} %param.8, f32[192,32,256]{2,1,0:T(8,128)} %fusion.125, bf16[192,32,256]{2,1,0:T(8,128)(2,1)S(1)} %copy.223), kind=kOutput, calls=%fused_computation.102 | convolution fusion | flops 4843765760 | bytes 47185920 | tf_op jit(solution)/shard_map/cwh,kh->cwk/dot_general | solution.py:26
  265.4 10.9 fusion.121
  276.3 7.5 subtract_convert_fusion.1
  295.4 10.9 fusion.117
  306.4 8.6 add_convert_fusion.2
  314.9 8.3 copy.230
  323.2 64.0 %all-to-all-done.2 = bf16[192,32,256]{0,1,2:T(8,128)(2,1)} async-done(((bf16[192,32,256]{0,1,2:T(8,128)(2,1)}), bf16[192,32,256]{0,1,2:T(8,128)(2,1)}, u32[]{:S(2)}, u32[]{:S(2)}) %all-to-all-start.2) | async-done | bytes 3145760 | tf_op jit(solution)/shard_map/all_to_all | solution.py:60
  405.7 7.5 copy.229
  413.3 71.0 %all-to-all-done.3 = bf16[192,32,256]{0,1,2:T(8,128)(2,1)} async-done(((bf16[192,32,256]{0,1,2:T(8,128)(2,1)}), bf16[192,32,256]{0,1,2:T(8,128)(2,1)}, u32[]{:S(2)}, u32[]{:S(2)}) %all-to-all-start.3) | async-done | bytes 3145760 | tf_op jit(solution)/shard_map/all_to_all | solution.py:63
  496.3 8.2 copy.233
  530.1 37.9 %fusion.253 = (bf16[192,32,256]{2,1,0:T(8,128)(2,1)S(1)}, f32[192,32,256]{2,1,0:T(8,128)}) fusion(f32[192]{0:T(256)S(1)} %bitcast.308, f32[192,34,256]{2,1,0:T(8,128)} %maximum_convert_fusion, f32[192]{0:T(256)S(1)} %bitcast.310, f32[192]{0:T(256)S(1)} %bitcast.296, f32[192]{0:T(256)S(1)} %bitcast.298, f32[192]{0:T(256)S(1)} %bitcast.300, ...), kind=kLoop, calls=%fused_computation.292 | loop fusion | flops 31457280 | bytes 39328512 | tf_op jit(solution)/shard_map/convert_element_type | solution.py:126
  579.2 7.4 copy.244
  593.7 9.8 reshape.83
  603.5 16.1 %fusion.261 = f32[3072,2048]{0,1} fusion(bf16[3072,768]{1,0:T(8,128)(2,1)} %all-gather.5.cloned.1.call-done, bf16[768,2048]{0,1:T(8,128)(2,1)S(1)} %reshape.95), kind=kOutput, calls=%fused_computation.297 | convolution fusion | flops 9663676416 | bytes 33030144
  619.5 7.9 all-to-all-done.4
  627.4 9.6 fusion.255
  637.1 13.8 copy.236
  650.9 10.2 reshape.84
  669.5 80.0 %fusion.7 = (bf16[3072,32,64]{0,2,1:T(8,128)(2,1)}, bf16[3072,32,64]{0,2,1:T(8,128)(2,1)}) fusion(f32[3072,32,64]{0,2,1:T(8,128)} %bitcast.313, bf16[768,3072]{1,0:T(8,128)(2,1)S(1)} %bitcast.292, f32[768,32,64]{0,2,1:T(8,128)S(1)} %subtract_multiply_fusion, f32[768]{0:T(1024)S(1)} %copy-done.33), kind=kOutput, calls=%fused_computation.9 | convolution fusion | flops 10138681344 | bytes 61344768 | tf_op jit(solution)/shard_map/chw,cf->fhw/dot_general | solution.py:137
  749.4 22.7 %bitcast_reduce_fusion = (f32[4,32,64]{2,1,0:T(8,128)S(1)}, f32[4,32,64]{2,1,0:T(8,128)S(1)}, f32[4,32,64,768]{3,2,1,0:T(8,128)}) fusion(f32[768]{0:T(1024)S(1)} %copy-done.33, f32[768,32,64]{0,2,1:T(8,128)} %copy-done.9, bf16[768,4,768,1]{2,1,0,3:T(4,128)(2,1)} %bitcast.293, bf16[32,8,4,8,768]{4,3,2,1,0:T(8,128)(2,1)} %bitcast.315), kind=kOutput, calls=%fused_computation.12 | convolution fusion | flops 9688825856 | bytes 48827392 | tf_op jit(solution)/shard_map/pjra,spj->psra/dot_general | solution.py:151
  772.2 16.0 %fusion.10 = bf16[4,768,32,64]{1,3,2,0:T(8,128)(2,1)} fusion(f32[4,32,64,768]{3,2,1,0:T(8,128)} %get-tuple-element.33, f32[4,32,64]{2,1,0:T(8,128)S(1)} %get-tuple-element.34, f32[768,32,64]{0,2,1:T(8,128)} %copy-done.9, f32[4,32,64]{2,1,0:T(8,128)S(1)} %get-tuple-element.35, f32[768]{0:T(1024)S(1)} %copy-done.33, f32[32,64]{1,0:T(8,128)S(1)} %copy-done.13), kind=kLoop, calls=%fused_computation.15 | loop fusion | flops 37748736 | bytes 44116992 | tf_op jit(solution)/shard_map/convert_element_type | solution.py:108
  788.2 7.3 reduce_sum.65
  795.5 9.7 copy.247
  811.7 40.3 %all_to_all.189 = bf16[4,2,196608]{2,1,0:T(2,128)(2,1)} all-to-all(bf16[4,2,196608]{2,1,0:T(2,128)(2,1)S(1)} %reshape.101), channel_id=1, replica_groups=mesh['rows'=8,'ch'=4] {'ch'}, dimensions={0} | all-to-all | bytes 6291456 | tf_op jit(solution)/shard_map/all_to_all | solution.py:117
  851.9 7.5 reshape.102
  866.4 7.6 reshape.90
  873.9 8.3 copy.249
  882.3 9.5 copy.250
  912.3 15.1 %fusion.57 = f32[192,32,256]{2,1,0:T(8,128)} fusion(f32[192,34,256]{2,1,0:T(8,128)S(1)} %maximum_convert_fusion.1, f32[192]{0:T(256)S(1)} %bitcast.309, f32[192]{0:T(256)S(1)} %bitcast.311, f32[192]{0:T(256)S(1)} %bitcast.297, f32[192]{0:T(256)S(1)} %bitcast.299, f32[192]{0:T(256)S(1)} %bitcast.301, f32[192]{0:T(256)S(1)} %bitcast.303, f32[192]{0:T(256)S(1)} %bitcast.305, ...), kind=kLoop, calls=%fused_computation.86 | loop fusion | flops 26738688 | bytes 33039360 | tf_op jit(solution)/shard_map/add | solution.py:79
  927.4 12.5 fusion.77
  950.5 12.5 convert_bitcast_fusion.2
  968.7 75.3 %all-to-all-done.9 = bf16[192,256,32]{0,2,1:T(8,128)(2,1)} async-done(((bf16[192,256,32]{0,2,1:T(8,128)(2,1)}), bf16[192,256,32]{0,2,1:T(8,128)(2,1)}, u32[]{:S(2)}, u32[]{:S(2)}) %all-to-all-start.9) | async-done | bytes 3145760 | tf_op jit(solution)/shard_map/all_to_all | solution.py:47
  1048.9 17.0 %convert_bitcast_fusion = bf16[4,768,32,64]{1,3,2,0:T(8,128)(2,1)} fusion(bf16[4,768,768,1]{2,1,3,0:T(8,128)(2,1)} %bitcast.312, bf16[32,8,4,8,768]{4,3,2,1,0:T(8,128)(2,1)} %bitcast.314), kind=kOutput, calls=%fused_computation.60 | convolution fusion | flops 9669967872 | bytes 29884416 | tf_op jit(solution)/shard_map/bfhw,bfc->bchw/dot_general | solution.py:140
  1065.9 7.3 reduce_sum.62
  1073.1 9.4 copy.238
  1082.6 7.7 reshape.99
  1107.7 33.9 %all-to-all-done.8 = bf16[192,256,32]{0,2,1:T(8,128)(2,1)} async-done(((bf16[192,256,32]{0,2,1:T(8,128)(2,1)}), bf16[192,256,32]{0,2,1:T(8,128)(2,1)}, u32[]{:S(2)}, u32[]{:S(2)}) %all-to-all-start.8) | async-done | bytes 3145760 | tf_op jit(solution)/shard_map/all_to_all | solution.py:44
  1158.8 8.3 fusion.114
  1167.2 9.2 convolution_subtract_fusion
  1176.4 23.1 %multiply_bitcast_fusion.1 = (f32[1,192,32,256]{3,2,1,0:T(8,128)}, f32[1,192,32,256]{3,2,1,0:T(8,128)}, f32[192,32,256]{2,1,0:T(8,128)}, f32[192,32,256]{2,1,0:T(8,128)}) fusion(f32[192,32,256]{2,1,0:T(8,128)} %convolution_subtract_fusion, f32[192,32,256]{2,1,0:T(8,128)S(1)} %bitcast.270, f32[192,32,256]{2,1,0:T(8,128)} %get-tuple-element.32, ...), kind=kOutput, calls=%fused_computation.110 | convolution fusion | flops 4857921536 | bytes 66060288 | tf_op jit(solution)/shard_map/cwh,kh->cwk/dot_general | solution.py:26
  1199.6 11.1 fusion.110
  1210.6 7.5 subtract_convert_fusion
  1229.3 10.9 fusion.106
  1240.3 8.6 add_convert_fusion
  1248.9 8.2 copy.265
  1257.0 66.3 %all-to-all-done.10 = bf16[192,32,256]{0,1,2:T(8,128)(2,1)} async-done(((bf16[192,32,256]{0,1,2:T(8,128)(2,1)}), bf16[192,32,256]{0,1,2:T(8,128)(2,1)}, u32[]{:S(2)}, u32[]{:S(2)}) %all-to-all-start.10) | async-done | bytes 3145760 | tf_op jit(solution)/shard_map/all_to_all | solution.py:60
  1328.4 7.5 reshape.100
  1342.8 7.6 reshape.89
  1350.4 8.3 copy.240
  1358.7 9.4 copy.241
  1368.1 7.6 add_convert_fusion.1
  1375.8 9.7 pad_maximum_fusion
  1392.2 7.5 copy.264
  1406.4 15.1 %all-to-all-done.11 = bf16[192,32,256]{0,1,2:T(8,128)(2,1)} async-done(((bf16[192,32,256]{0,1,2:T(8,128)(2,1)}), bf16[192,32,256]{0,1,2:T(8,128)(2,1)}, u32[]{:S(2)}, u32[]{:S(2)}) %all-to-all-start.11) | async-done | bytes 3145760 | tf_op jit(solution)/shard_map/all_to_all | solution.py:63
  1428.5 8.3 copy.268
  1436.8 12.0 multiply_add_fusion
  (159 shorter events, 267.5 us)
Async XLA Ops:
  17.2 15.7 %copy-start.11 = (bf16[192,32,256]{2,1,0:T(8,128)(2,1)S(1)}, bf16[192,32,256]{2,1,0:T(8,128)(2,1)}, u32[]{:S(2)}) copy-start(bf16[192,32,256]{2,1,0:T(8,128)(2,1)} %param.7) | copy-start | bytes 9437188
  24.9 101.1 %all-to-all-start.1 = ((bf16[192,256,32]{0,2,1:T(8,128)(2,1)}), bf16[192,256,32]{0,2,1:T(8,128)(2,1)}, u32[]{:S(2)}, u32[]{:S(2)}) async-start(bf16[192,256,32]{0,2,1:T(8,128)(2,1)} %copy.221), calls=%async_computation.1 | async-start | bytes 8388608 | tf_op jit(solution)/shard_map/all_to_all | solution.py:47
  126.0 97.3 %all-to-all-start = ((bf16[192,256,32]{0,2,1:T(8,128)(2,1)}), bf16[192,256,32]{0,2,1:T(8,128)(2,1)}, u32[]{:S(2)}, u32[]{:S(2)}) async-start(bf16[192,256,32]{0,2,1:T(8,128)(2,1)} %copy.217), calls=%async_computation | async-start | bytes 8388608 | tf_op jit(solution)/shard_map/all_to_all | solution.py:44
  235.3 8.3 copy-start.6
  235.3 8.3 copy-start.8
  265.4 10.9 copy-start.1
  290.1 97.1 %all-to-all-start.2 = ((bf16[192,32,256]{0,1,2:T(8,128)(2,1)}), bf16[192,32,256]{0,1,2:T(8,128)(2,1)}, u32[]{:S(2)}, u32[]{:S(2)}) async-start(bf16[192,32,256]{0,1,2:T(8,128)(2,1)} %copy.226), calls=%async_computation.2 | async-start | bytes 8388608 | tf_op jit(solution)/shard_map/all_to_all | solution.py:60
  294.7 299.0 %all-gather.3.cloned.1.call-start = ((), (), s32[]{:S(2)}) async-start(), calls=%async_computation.12 | async-start | bytes 5898240 | tf_op jit(solution)/shard_map/all_gather | solution.py:129
  294.9 11.4 slice-start.4
  295.4 10.9 slice-start.5
  323.2 69.3 %copy-start.3 = (bf16[192,32,256]{2,1,0:T(8,128)(2,1)S(1)}, bf16[192,32,256]{2,1,0:T(8,128)(2,1)}, u32[]{:S(2)}) copy-start(bf16[192,32,256]{2,1,0:T(8,128)(2,1)} %param.13) | copy-start | bytes 9437188
  387.2 97.1 %all-to-all-start.3 = ((bf16[192,32,256]{0,1,2:T(8,128)(2,1)}), bf16[192,32,256]{0,1,2:T(8,128)(2,1)}, u32[]{:S(2)}, u32[]{:S(2)}) async-start(bf16[192,32,256]{0,1,2:T(8,128)(2,1)} %copy.230), calls=%async_computation.3 | async-start | bytes 8388608 | tf_op jit(solution)/shard_map/all_to_all | solution.py:63
  391.8 211.7 %all-gather.5.cloned.1.call-start = ((), (), s32[]{:S(2)}) async-start(), calls=%async_computation.13 | async-start | bytes 5898240 | tf_op jit(solution)/shard_map/all_gather | solution.py:130
  484.3 90.1 %all-to-all-start.6 = ((bf16[192,32,256]{0,1,2:T(8,128)(2,1)}), bf16[192,32,256]{0,1,2:T(8,128)(2,1)}, u32[]{:S(2)}, u32[]{:S(2)}) async-start(bf16[192,32,256]{0,1,2:T(8,128)(2,1)} %copy.242), calls=%async_computation.6 | async-start | bytes 8388608 | tf_op jit(solution)/shard_map/all_to_all | solution.py:113
  504.5 3.8 copy-start.10
  508.4 10.2 copy-start.32
  512.5 9.2 collective-permute-start.1
  513.8 12.0 collective-permute-start
  518.6 49.4 %copy-start.14 = (f32[192,1]{0,1:T(1,128)}, f32[192,1]{0,1:T(1,128)S(1)}, u32[]{:S(2)}) copy-start(f32[192,1]{0,1:T(1,128)S(1)} %get-tuple-element.23) | copy-start | bytes 2308
  518.6 49.4 %copy-start.16 = (f32[192,1]{0,1:T(1,128)}, f32[192,1]{0,1:T(1,128)S(1)}, u32[]{:S(2)}) copy-start(f32[192,1]{0,1:T(1,128)S(1)} %get-tuple-element.24) | copy-start | bytes 2308
  518.6 49.4 %copy-start.18 = (f32[192,1]{0,1:T(1,128)}, f32[192,1]{0,1:T(1,128)S(1)}, u32[]{:S(2)}) copy-start(f32[192,1]{0,1:T(1,128)S(1)} %get-tuple-element.25) | copy-start | bytes 2308
  518.6 49.4 %copy-start.20 = (f32[192,1]{0,1:T(1,128)}, f32[192,1]{0,1:T(1,128)S(1)}, u32[]{:S(2)}) copy-start(f32[192,1]{0,1:T(1,128)S(1)} %get-tuple-element.26) | copy-start | bytes 2308
  518.6 49.4 %copy-start.22 = (f32[192,1]{0,1:T(1,128)}, f32[192,1]{0,1:T(1,128)S(1)}, u32[]{:S(2)}) copy-start(f32[192,1]{0,1:T(1,128)S(1)} %get-tuple-element.27) | copy-start | bytes 2308
  518.6 49.4 %copy-start.24 = (f32[192,1]{0,1:T(1,128)}, f32[192,1]{0,1:T(1,128)S(1)}, u32[]{:S(2)}) copy-start(f32[192,1]{0,1:T(1,128)S(1)} %get-tuple-element.28) | copy-start | bytes 2308
  518.6 49.4 %copy-start.26 = (f32[192,1]{0,1:T(1,128)}, f32[192,1]{0,1:T(1,128)S(1)}, u32[]{:S(2)}) copy-start(f32[192,1]{0,1:T(1,128)S(1)} %get-tuple-element.29) | copy-start | bytes 2308
  518.6 49.4 %copy-start.28 = (f32[192,1]{0,1:T(1,128)}, f32[192,1]{0,1:T(1,128)S(1)}, u32[]{:S(2)}) copy-start(f32[192,1]{0,1:T(1,128)S(1)} %get-tuple-element.30) | copy-start | bytes 2308
  518.6 49.4 %copy-start.30 = (f32[192,1]{0,1:T(1,128)}, f32[192,1]{0,1:T(1,128)S(1)}, u32[]{:S(2)}) copy-start(f32[192,1]{0,1:T(1,128)S(1)} %get-tuple-element.31) | copy-start | bytes 2308
  574.4 53.1 %all-to-all-start.4 = ((bf16[192,32,256]{0,1,2:T(8,128)(2,1)}), bf16[192,32,256]{0,1,2:T(8,128)(2,1)}, u32[]{:S(2)}, u32[]{:S(2)}) async-start(bf16[192,32,256]{0,1,2:T(8,128)(2,1)} %copy.234), calls=%async_computation.4 | async-start | bytes 8388608 | tf_op jit(solution)/shard_map/all_to_all | solution.py:113
  661.1 3.5 copy-start.2
  664.5 4.9 slice-start.8
  666.1 3.3 copy-start.12
  666.1 3.3 slice-start.9
  666.1 3.3 copy-start.33
  669.4 80.0 %copy-start.9 = (f32[768,32,64]{0,2,1:T(8,128)}, f32[768,32,64]{0,2,1:T(8,128)S(1)}, u32[]{:S(2)}) copy-start(f32[768,32,64]{0,2,1:T(8,128)S(1)} %subtract_multiply_fusion) | copy-start | bytes 18874372
  749.4 22.7 %copy-start.13 = (f32[32,64]{1,0:T(8,128)S(1)}, f32[32,64]{1,0:T(8,128)}, u32[]{:S(2)}) copy-start(f32[32,64]{1,0:T(8,128)} %copy-done.12) | copy-start | bytes 24580
  882.3 9.6 copy-start.4
  895.8 16.4 %copy-start.15 = (f32[192,1]{0,1:T(1,128)S(1)}, f32[192,1]{0,1:T(1,128)}, u32[]{:S(2)}) copy-start(f32[192,1]{0,1:T(1,128)} %copy-done.14) | copy-start | bytes 2308
  895.8 16.4 %copy-start.17 = (f32[192,1]{0,1:T(1,128)S(1)}, f32[192,1]{0,1:T(1,128)}, u32[]{:S(2)}) copy-start(f32[192,1]{0,1:T(1,128)} %copy-done.16) | copy-start | bytes 2308
  895.8 16.4 %copy-start.19 = (f32[192,1]{0,1:T(1,128)S(1)}, f32[192,1]{0,1:T(1,128)}, u32[]{:S(2)}) copy-start(f32[192,1]{0,1:T(1,128)} %copy-done.18) | copy-start | bytes 2308
  895.9 16.4 %copy-start.21 = (f32[192,1]{0,1:T(1,128)S(1)}, f32[192,1]{0,1:T(1,128)}, u32[]{:S(2)}) copy-start(f32[192,1]{0,1:T(1,128)} %copy-done.20) | copy-start | bytes 2308
  895.9 16.4 %copy-start.23 = (f32[192,1]{0,1:T(1,128)S(1)}, f32[192,1]{0,1:T(1,128)}, u32[]{:S(2)}) copy-start(f32[192,1]{0,1:T(1,128)} %copy-done.22) | copy-start | bytes 2308
  895.9 16.4 %copy-start.25 = (f32[192,1]{0,1:T(1,128)S(1)}, f32[192,1]{0,1:T(1,128)}, u32[]{:S(2)}) copy-start(f32[192,1]{0,1:T(1,128)} %copy-done.24) | copy-start | bytes 2308
  895.9 16.4 %copy-start.27 = (f32[192,1]{0,1:T(1,128)S(1)}, f32[192,1]{0,1:T(1,128)}, u32[]{:S(2)}) copy-start(f32[192,1]{0,1:T(1,128)} %copy-done.26) | copy-start | bytes 2308
  895.9 16.4 %copy-start.29 = (f32[192,1]{0,1:T(1,128)S(1)}, f32[192,1]{0,1:T(1,128)}, u32[]{:S(2)}) copy-start(f32[192,1]{0,1:T(1,128)} %copy-done.28) | copy-start | bytes 2308
  895.9 16.4 %copy-start.31 = (f32[192,1]{0,1:T(1,128)S(1)}, f32[192,1]{0,1:T(1,128)}, u32[]{:S(2)}) copy-start(f32[192,1]{0,1:T(1,128)} %copy-done.30) | copy-start | bytes 2308
  896.2 8.9 collective-permute-start.3
  897.5 12.0 collective-permute-start.2
  945.7 98.4 %all-to-all-start.9 = ((bf16[192,256,32]{0,2,1:T(8,128)(2,1)}), bf16[192,256,32]{0,2,1:T(8,128)(2,1)}, u32[]{:S(2)}, u32[]{:S(2)}) async-start(bf16[192,256,32]{0,2,1:T(8,128)(2,1)} %copy.256), calls=%async_computation.9 | async-start | bytes 8388608 | tf_op jit(solution)/shard_map/all_to_all | solution.py:47
  1044.1 97.6 %all-to-all-start.8 = ((bf16[192,256,32]{0,2,1:T(8,128)(2,1)}), bf16[192,256,32]{0,2,1:T(8,128)(2,1)}, u32[]{:S(2)}, u32[]{:S(2)}) async-start(bf16[192,256,32]{0,2,1:T(8,128)(2,1)} %copy.252), calls=%async_computation.8 | async-start | bytes 8388608 | tf_op jit(solution)/shard_map/all_to_all | solution.py:44
  1141.6 82.8 %all-to-all-start.5 = ((bf16[4,2,196608]{2,1,0:T(2,128)(2,1)}), bf16[4,2,196608]{2,1,0:T(2,128)(2,1)}, u32[]{:S(2)}, u32[]{:S(2)}) async-start(bf16[4,2,196608]{2,1,0:T(2,128)(2,1)} %reshape.99), calls=%async_computation.5 | async-start | bytes 6291456 | tf_op jit(solution)/shard_map/all_to_all | solution.py:117
  1158.8 8.3 copy-start.7
  1158.8 17.6 %slice-start = ((s8[6291456]{0:T(1024)(128)(4,1)}), s8[4194304]{0:T(1024)(128)(4,1)S(1)}, s32[]{:S(2)}) async-start(s8[6291456]{0:T(1024)(128)(4,1)} %bitcast.269), calls=%async_computation.14 | async-start | bytes 8388608
  1167.2 9.3 slice-start.1
  1199.5 11.1 copy-start
  1224.4 15.8 %slice-start.2 = ((s8[6291456]{0:T(1024)(128)(4,1)}), s8[2097152]{0:T(1024)(128)(4,1)S(1)}, s32[]{:S(2)}) async-start(s8[6291456]{0:T(1024)(128)(4,1)} %bitcast.271), calls=%async_computation.16 | async-start | bytes 4194304
  1224.4 99.0 %all-to-all-start.10 = ((bf16[192,32,256]{0,1,2:T(8,128)(2,1)}), bf16[192,32,256]{0,1,2:T(8,128)(2,1)}, u32[]{:S(2)}, u32[]{:S(2)}) async-start(bf16[192,32,256]{0,1,2:T(8,128)(2,1)} %copy.261), calls=%async_computation.10 | async-start | bytes 8388608 | tf_op jit(solution)/shard_map/all_to_all | solution.py:60
  1229.3 10.9 slice-start.3
  1323.4 98.2 %all-to-all-start.11 = ((bf16[192,32,256]{0,1,2:T(8,128)(2,1)}), bf16[192,32,256]{0,1,2:T(8,128)(2,1)}, u32[]{:S(2)}, u32[]{:S(2)}) async-start(bf16[192,32,256]{0,1,2:T(8,128)(2,1)} %copy.265), calls=%async_computation.11 | async-start | bytes 8388608 | tf_op jit(solution)/shard_map/all_to_all | solution.py:63
  1358.7 17.0 %slice-start.6 = ((s8[6291456]{0:T(1024)(128)(4,1)}), s8[2097152]{0:T(1024)(128)(4,1)S(1)}, s32[]{:S(2)}) async-start(s8[6291456]{0:T(1024)(128)(4,1)} %bitcast.281), calls=%async_computation.20 | async-start | bytes 4194304
  1368.1 7.6 slice-start.7
  1421.6 15.2 %copy-start.5 = (bf16[192,32,256]{2,1,0:T(8,128)(2,1)S(1)}, bf16[192,32,256]{2,1,0:T(8,128)(2,1)}, u32[]{:S(2)}) copy-start(bf16[192,32,256]{2,1,0:T(8,128)(2,1)} %param.13) | copy-start | bytes 9437188
Sparse Core Ops, SparseCore 0:
  297.1 38.7 all-gather.2
  394.2 38.7 all-gather.4
where the time goes:
time: 1470 us; the launch traced here: 1460 us
  waiting for transfers between devices  501 us (34%)
  matrix products  365 us (25%)
  local copies, waits for them, and re-layouts  336 us (23%)
  other arithmetic  129 us (9%)
  starting transfers between devices  69.1 us (5%)
  blocking collectives  40.3 us (3%)
  between operations  15.2 us (1%)
    dot_general x24, matrix products, contract(): jnp.einsum(form, left, right, precision=lax.Precision.HIGHEST, preferred_...  229 us
    all_to_all x2, waiting for transfers between devices, filter_pass(): lax.all_to_all(head_im.astype(jnp.bfloat16), 'rows', split_axis=1, concat...  153 us
    all_to_all x2, waiting for transfers between devices, filter_pass(): lax.all_to_all(back_re.astype(jnp.bfloat16), 'rows', split_axis=2, concat...  130 us
    all_to_all x2, waiting for transfers between devices, filter_pass(): lax.all_to_all(head_re.astype(jnp.bfloat16), 'rows', split_axis=1, concat...  109 us
    all_to_all x2, waiting for transfers between devices, filter_pass(): lax.all_to_all(back_im.astype(jnp.bfloat16), 'rows', split_axis=2, concat...  86.2 us
    dot_general x1, matrix products, on_device(): jnp.einsum('chw,cf->fhw', scaled, full_up, preferred_element_type=jnp.flo...  80 us
    convert_element_type x6, local copies, waits for them, and re-layouts, to_channels(): return lax.all_to_all(values.astype(jnp.bfloat16), 'ch', split_axis=0, co...  50.7 us
    unnamed x94, local copies, waits for them, and re-layouts  43.1 us
  transfers between devices with their start and end apart: 17, of which 13 were waited for; matrix products, arithmetic and copies ran while one was open for 31% of the time, Pallas kernels for 0%

commit v1 on v0

--- a/solution.py
+++ b/solution.py
@@ -1,3 +1,4 @@
+import functools
 import math
 import jax
 import jax.numpy as jnp
@@ -7,6 +8,34 @@
 norm_epsilon = 1e-05
 root_half = 0.7071067811865476
 density = 0.3989422804014327
+
+
+def arrays_search(vector, dim_no, vec):
+    latest = vector.shape
+    passed = vector.reshape(*latest[:dim_no], vec, latest[dim_no] // vec, *latest[dim_no + 1 :])
+    return jnp.moveaxis(passed, dim_no, 0)
+
+
+def _detail_files(work_x, axis_no):
+    moved = list(work_x.shape[1:])
+    moved[axis_no] *= work_x.shape[0]
+    return jnp.moveaxis(work_x, 0, axis_no).reshape(moved)
+
+
+def _review_steps_all(mine, axis_name, inner_x, array_here):
+    part_now, known = (lax.axis_size(axis_name), lax.axis_index(axis_name))
+    z2 = arrays_search(mine, inner_x, part_now)
+    items = [z2[known]]
+    for s in range(1, part_now):
+        local_now = z2[(known + s) % part_now]
+        items.append(
+            lax.ppermute(local_now, axis_name, [(h, (h + s) % part_now) for h in range(part_now)])
+        )
+    z2 = jnp.stack(items, axis=0)[(known - jnp.arange(part_now)) % part_now]
+    return _detail_files(z2, array_here)
+
+
+change_digits = functools.partial(_review_steps_all, axis_name="rows", inner_x=2, array_here=1)
 
 
 def with_halo(block, sides, width):
@@ -60,9 +89,7 @@
         lax.all_to_all(
             back_re.astype(jnp.bfloat16), "rows", split_axis=2, concat_axis=1, tiled=True
         ).astype(back_re.dtype),
-        lax.all_to_all(
-            back_im.astype(jnp.bfloat16), "rows", split_axis=2, concat_axis=1, tiled=True
-        ).astype(back_im.dtype),
+        change_digits(back_im.astype(jnp.bfloat16)).astype(back_im.dtype),
     )
     outcome = contract("ckh,kw->chw", row_re, cos_w) - contract("ckh,kw->chw", row_im, sin_w)
     return (outcome * (1.0 / (row_len * col_len)), spec_re, spec_im)

time: 1470 us -> 1480 us (level)
  the two profiles are of different devices: /device:TPU:0 before, /device:TPU:31 now
where the time goes in v1:
time: 1480 us; the launch traced here: 1470 us
  waiting for transfers between devices  392 us (26%)
  matrix products  357 us (24%)
  local copies, waits for them, and re-layouts  355 us (24%)
  starting transfers between devices  180 us (12%)
  other arithmetic  132 us (9%)
  blocking collectives  40.3 us (3%)
  between operations  15.3 us (1%)
    dot_general x24, matrix products, contract(): jnp.einsum(form, left, right, precision=lax.Precision.HIGHEST, preferred_...  221 us
    all_to_all x2, waiting for transfers between devices, filter_pass(): lax.all_to_all(head_im.astype(jnp.bfloat16), 'rows', split_axis=1, concat...  149 us
    ppermute x14, starting transfers between devices, _review_steps_all(): lax.ppermute(local_now, axis_name, [(h, (h + s) % part_now) for h in rang...  115 us
    all_to_all x2, waiting for transfers between devices, filter_pass(): lax.all_to_all(head_re.astype(jnp.bfloat16), 'rows', split_axis=1, concat...  113 us
    ppermute x14, waiting for transfers between devices, _review_steps_all(): lax.ppermute(local_now, axis_name, [(h, (h + s) % part_now) for h in rang...  111 us
    dot_general x1, matrix products, on_device(): jnp.einsum('chw,cf->fhw', scaled, full_up, preferred_element_type=jnp.flo...  79.9 us
    unnamed x106, local copies, waits for them, and re-layouts  58.8 us
    convert_element_type x6, local copies, waits for them, and re-layouts, to_channels(): return lax.all_to_all(values.astype(jnp.bfloat16), 'ch', split_axis=0, co...  50.8 us
  transfers between devices with their start and end apart: 29, of which 13 were waited for; matrix products, arithmetic and copies ran while one was open for 36% of the time, Pallas kernels for 0%

profile of v1, /device:TPU:31, one launch (start us, length us, event | category | flops | bytes accessed | tf_op | source)
XLA Modules:
  0.0 1471.9 jit_solution(15930954526008901719)
XLA Ops:
  7.2 10.0 fusion.76
  17.2 7.8 copy.207
  30.9 8.2 convert_bitcast_fusion.3
  39.1 7.6 copy.203
  46.7 75.8 %all-to-all-done.1 = bf16[192,256,32]{0,2,1:T(8,128)(2,1)} async-done(((bf16[192,256,32]{0,2,1:T(8,128)(2,1)}), bf16[192,256,32]{0,2,1:T(8,128)(2,1)}, u32[]{:S(2)}, u32[]{:S(2)}) %all-to-all-start.1) | async-done | bytes 3145760 | tf_op jit(solution)/shard_map/all_to_all | solution.py:76
  139.7 79.9 %all-to-all-done = bf16[192,256,32]{0,2,1:T(8,128)(2,1)} async-done(((bf16[192,256,32]{0,2,1:T(8,128)(2,1)}), bf16[192,256,32]{0,2,1:T(8,128)(2,1)}, u32[]{:S(2)}, u32[]{:S(2)}) %all-to-all-start) | async-done | bytes 3145760 | tf_op jit(solution)/shard_map/all_to_all | solution.py:73
  248.2 15.1 %fusion.64 = (f32[192,32,256]{2,1,0:T(8,128)}, f32[192,32,256]{2,1,0:T(8,128)}, f32[192,32,256]{2,1,0:T(8,128)}) fusion(f32[192,32,256]{2,1,0:T(8,128)} %convolution_subtract_fusion.1, f32[2,192,32,256]{3,2,1,0:T(8,128)} %param.8, f32[192,32,256]{2,1,0:T(8,128)} %fusion.125, bf16[192,32,256]{2,1,0:T(8,128)(2,1)S(1)} %copy.209), kind=kOutput, calls=%fused_computation.104 | convolution fusion | flops 4843765760 | bytes 47185920 | tf_op jit(solution)/shard_map/cwh,kh->cwk/dot_general | solution.py:55
  263.3 10.9 fusion.121
  274.2 7.5 subtract_convert_fusion.1
  294.3 11.0 fusion.117
  305.3 8.6 add_convert_fusion.2
  313.9 7.3 copy.216
  338.3 32.8 %collective-permute-done = bf16[192,32,32]{0,2,1:T(8,128)(2,1)} collective-permute-done((bf16[192,32,32]{0,2,1:T(8,128)(2,1)}, bf16[192,32,32]{0,2,1:T(8,128)(2,1)}, u32[]{:S(2)}, u32[]{:S(2)}) %collective-permute-start) | collective-permute-done | bytes 393248 | tf_op jit(solution)/shard_map/ppermute | solution.py:32
  372.9 9.4 collective-permute-done.1
  382.3 62.4 %collective-permute-start.6 = (bf16[192,32,32]{0,2,1:T(8,128)(2,1)}, bf16[192,32,32]{0,2,1:T(8,128)(2,1)S(1)}, u32[]{:S(2)}, u32[]{:S(2)}) collective-permute-start(bf16[192,32,32]{0,2,1:T(8,128)(2,1)} %get-tuple-element.26), channel_id=1, source_target_pairs={{0,28},{4,0},{8,4},{12,8},{16,12},{20,16},{24,20},{28,24},{1,29},{... | collective-permute-start | bytes 1179656 | tf_op jit(solution)/shard_map/ppermute | solution.py:32
  447.3 27.6 %collective-permute-done.3 = bf16[192,32,32]{0,2,1:T(8,128)(2,1)S(1)} collective-permute-done((bf16[192,32,32]{0,2,1:T(8,128)(2,1)}, bf16[192,32,32]{0,2,1:T(8,128)(2,1)S(1)}, u32[]{:S(2)}, u32[]{:S(2)}) %collective-permute-start.3) | collective-permute-done | bytes 393248 | tf_op jit(solution)/shard_map/ppermute | solution.py:32
  483.2 7.5 copy.217
  503.2 8.2 copy.215
  535.2 37.9 %fusion.255 = (bf16[192,32,256]{2,1,0:T(8,128)(2,1)S(1)}, f32[192,32,256]{2,1,0:T(8,128)}) fusion(f32[192]{0:T(256)S(1)} %bitcast.374, f32[192,34,256]{2,1,0:T(8,128)} %maximum_convert_fusion, f32[192]{0:T(256)S(1)} %bitcast.376, f32[192]{0:T(256)S(1)} %bitcast.362, f32[192]{0:T(256)S(1)} %bitcast.364, f32[192]{0:T(256)S(1)} %bitcast.366, ...), kind=kLoop, calls=%fused_computation.331 | loop fusion | flops 31457280 | bytes 39328512 | tf_op jit(solution)/shard_map/convert_element_type | solution.py:153
  585.2 7.4 copy.228
  599.7 9.7 reshape.176
  609.4 15.8 %fusion.263 = f32[3072,2048]{0,1} fusion(bf16[3072,768]{1,0:T(8,128)(2,1)} %all-gather.5.cloned.1.call-done, bf16[768,2048]{0,1:T(8,128)(2,1)S(1)} %reshape.206), kind=kOutput, calls=%fused_computation.336 | convolution fusion | flops 9663676416 | bytes 33030144
  631.6 9.6 fusion.257
  641.2 13.8 copy.220
  655.0 10.2 reshape.179
  673.6 79.9 %fusion.7 = (bf16[3072,32,64]{0,2,1:T(8,128)(2,1)}, bf16[3072,32,64]{0,2,1:T(8,128)(2,1)}) fusion(f32[3072,32,64]{0,2,1:T(8,128)} %bitcast.379, bf16[768,3072]{1,0:T(8,128)(2,1)S(1)} %bitcast.358, f32[768,32,64]{0,2,1:T(8,128)S(1)} %subtract_multiply_fusion, f32[768]{0:T(1024)S(1)} %copy-done.32), kind=kOutput, calls=%fused_computation.11 | convolution fusion | flops 10138681344 | bytes 61344768 | tf_op jit(solution)/shard_map/chw,cf->fhw/dot_general | solution.py:164
  753.6 22.7 %bitcast_reduce_fusion = (f32[4,32,64]{2,1,0:T(8,128)S(1)}, f32[4,32,64]{2,1,0:T(8,128)S(1)}, f32[4,32,64,768]{3,2,1,0:T(8,128)}) fusion(f32[768]{0:T(1024)S(1)} %copy-done.32, f32[768,32,64]{0,2,1:T(8,128)} %copy-done.8, bf16[768,4,768,1]{2,1,0,3:T(4,128)(2,1)} %bitcast.359, bf16[32,8,4,8,768]{4,3,2,1,0:T(8,128)(2,1)} %bitcast.381), kind=kOutput, calls=%fused_computation.14 | convolution fusion | flops 9688825856 | bytes 48827392 | tf_op jit(solution)/shard_map/pjra,spj->psra/dot_general | solution.py:178
  776.3 16.1 %fusion.10 = bf16[4,768,32,64]{1,3,2,0:T(8,128)(2,1)} fusion(f32[4,32,64,768]{3,2,1,0:T(8,128)} %get-tuple-element.47, f32[4,32,64]{2,1,0:T(8,128)S(1)} %get-tuple-element.48, f32[768,32,64]{0,2,1:T(8,128)} %copy-done.8, f32[4,32,64]{2,1,0:T(8,128)S(1)} %get-tuple-element.49, f32[768]{0:T(1024)S(1)} %copy-done.32, f32[32,64]{1,0:T(8,128)S(1)} %copy-done.11), kind=kLoop, calls=%fused_computation.17 | loop fusion | flops 37748736 | bytes 44116992 | tf_op jit(solution)/shard_map/convert_element_type | solution.py:135
  792.4 7.3 reduce_sum.65
  799.7 9.8 copy.231
  816.1 40.3 %all_to_all.153 = bf16[4,2,196608]{2,1,0:T(2,128)(2,1)} all-to-all(bf16[4,2,196608]{2,1,0:T(2,128)(2,1)S(1)} %reshape.212), channel_id=1, replica_groups=mesh['rows'=8,'ch'=4] {'ch'}, dimensions={0} | all-to-all | bytes 6291456 | tf_op jit(solution)/shard_map/all_to_all | solution.py:144
  856.3 7.5 reshape.213
  870.8 7.6 reshape.185
  878.4 8.4 copy.233
  886.7 9.6 copy.234
  914.9 15.1 %fusion.57 = f32[192,32,256]{2,1,0:T(8,128)} fusion(f32[192,34,256]{2,1,0:T(8,128)S(1)} %maximum_convert_fusion.1, f32[192]{0:T(256)S(1)} %bitcast.375, f32[192]{0:T(256)S(1)} %bitcast.377, f32[192]{0:T(256)S(1)} %bitcast.363, f32[192]{0:T(256)S(1)} %bitcast.365, f32[192]{0:T(256)S(1)} %bitcast.367, f32[192]{0:T(256)S(1)} %bitcast.369, f32[192]{0:T(256)S(1)} %bitcast.371, ...), kind=kLoop, calls=%fused_computation.88 | loop fusion | flops 26738688 | bytes 33039360 | tf_op jit(solution)/shard_map/add | solution.py:106
  930.0 12.5 fusion.77
  948.2 9.2 all-to-all-start.8
  957.4 12.5 convert_bitcast_fusion.2
  975.6 73.4 %all-to-all-done.8 = bf16[192,256,32]{0,2,1:T(8,128)(2,1)} async-done(((bf16[192,256,32]{0,2,1:T(8,128)(2,1)}), bf16[192,256,32]{0,2,1:T(8,128)(2,1)}, u32[]{:S(2)}, u32[]{:S(2)}) %all-to-all-start.8) | async-done | bytes 3145760 | tf_op jit(solution)/shard_map/all_to_all | solution.py:76
  1054.9 17.0 %convert_bitcast_fusion = bf16[4,768,32,64]{1,3,2,0:T(8,128)(2,1)} fusion(bf16[4,768,768,1]{2,1,3,0:T(8,128)(2,1)} %bitcast.378, bf16[32,8,4,8,768]{4,3,2,1,0:T(8,128)(2,1)} %bitcast.380), kind=kOutput, calls=%fused_computation.62 | convolution fusion | flops 9669967872 | bytes 29884416 | tf_op jit(solution)/shard_map/bfhw,bfc->bchw/dot_general | solution.py:167
  1071.9 7.3 reduce_sum.62
  1079.1 9.4 copy.222
  1088.6 7.7 reshape.210
  1113.8 32.7 %all-to-all-done.7 = bf16[192,256,32]{0,2,1:T(8,128)(2,1)} async-done(((bf16[192,256,32]{0,2,1:T(8,128)(2,1)}), bf16[192,256,32]{0,2,1:T(8,128)(2,1)}, u32[]{:S(2)}, u32[]{:S(2)}) %all-to-all-start.7) | async-done | bytes 3145760 | tf_op jit(solution)/shard_map/all_to_all | solution.py:73
  1164.7 8.2 fusion.114
  1172.9 9.3 convolution_subtract_fusion
  1182.2 23.1 %multiply_bitcast_fusion.1 = (f32[1,192,32,256]{3,2,1,0:T(8,128)}, f32[1,192,32,256]{3,2,1,0:T(8,128)}, f32[192,32,256]{2,1,0:T(8,128)}, f32[192,32,256]{2,1,0:T(8,128)}) fusion(f32[192,32,256]{2,1,0:T(8,128)} %convolution_subtract_fusion, f32[192,32,256]{2,1,0:T(8,128)S(1)} %bitcast.334, f32[192,32,256]{2,1,0:T(8,128)} %get-tuple-element.46, ...), kind=kOutput, calls=%fused_computation.112 | convolution fusion | flops 4857921536 | bytes 66060288 | tf_op jit(solution)/shard_map/cwh,kh->cwk/dot_general | solution.py:55
  1205.3 11.1 fusion.110
  1216.4 7.5 subtract_convert_fusion
  1237.2 7.5 reshape.211
  1251.7 7.6 reshape.184
  1259.2 8.4 copy.224
  1267.6 9.4 copy.225
  1277.0 7.6 add_convert_fusion.1
  1284.6 10.7 fusion.106
  1295.3 8.8 add_convert_fusion
  1318.7 12.1 pad_maximum_fusion
  1337.9 11.1 collective-permute-done.12
  1349.0 38.2 %collective-permute-start.17 = (bf16[192,32,32]{0,2,1:T(8,128)(2,1)S(1)}, bf16[192,32,32]{0,2,1:T(8,128)(2,1)S(1)}, u32[]{:S(2)}, u32[]{:S(2)}) collective-permute-start(bf16[192,32,32]{0,2,1:T(8,128)(2,1)S(1)} %get-tuple-element.17), channel_id=1, source_target_pairs={{0,28},{4,0},{8,4},{12,8},{16,12},{20,16},{24,20},{28,24},{1,29},{... | collective-permute-start | bytes 1179656 | tf_op jit(solution)/shard_map/ppermute | solution.py:32
  1388.8 29.7 %collective-permute-done.14 = bf16[192,32,32]{0,2,1:T(8,128)(2,1)S(1)} collective-permute-done((bf16[192,32,32]{0,2,1:T(8,128)(2,1)S(1)}, bf16[192,32,32]{0,2,1:T(8,128)(2,1)S(1)}, u32[]{:S(2)}, u32[]{:S(2)}) %collective-permute-start.14) | collective-permute-done | bytes 393248 | tf_op jit(solution)/shard_map/ppermute | solution.py:32
  1427.0 8.5 copy.250
  1442.3 8.4 copy.248
  1456.4 8.4 multiply_add_fusion
  (201 shorter events, 313.0 us)
Async XLA Ops:
  17.2 13.7 copy-start.9
  24.9 97.6 %all-to-all-start.1 = ((bf16[192,256,32]{0,2,1:T(8,128)(2,1)}), bf16[192,256,32]{0,2,1:T(8,128)(2,1)}, u32[]{:S(2)}, u32[]{:S(2)}) async-start(bf16[192,256,32]{0,2,1:T(8,128)(2,1)} %copy.207), calls=%async_computation.1 | async-start | bytes 8388608 | tf_op jit(solution)/shard_map/all_to_all | solution.py:76
  122.5 97.1 %all-to-all-start = ((bf16[192,256,32]{0,2,1:T(8,128)(2,1)}), bf16[192,256,32]{0,2,1:T(8,128)(2,1)}, u32[]{:S(2)}, u32[]{:S(2)}) async-start(bf16[192,256,32]{0,2,1:T(8,128)(2,1)} %copy.203), calls=%async_computation | async-start | bytes 8388608 | tf_op jit(solution)/shard_map/all_to_all | solution.py:73
  127.9 471.7 %all-gather.3.cloned.1.call-start = ((), (), s32[]{:S(2)}) async-start(), calls=%async_computation.10 | async-start | bytes 5898240 | tf_op jit(solution)/shard_map/all_gather | solution.py:156
  263.3 10.9 copy-start
  288.0 202.8 %all-to-all-start.2 = ((bf16[192,32,256]{0,1,2:T(8,128)(2,1)}), bf16[192,32,256]{0,1,2:T(8,128)(2,1)}, u32[]{:S(2)}, u32[]{:S(2)}) async-start(bf16[192,32,256]{0,1,2:T(8,128)(2,1)} %copy.212), calls=%async_computation.2 | async-start | bytes 8388608 | tf_op jit(solution)/shard_map/all_to_all | solution.py:89
  293.4 316.0 %all-gather.5.cloned.1.call-start = ((), (), s32[]{:S(2)}) async-start(), calls=%async_computation.11 | async-start | bytes 5898240 | tf_op jit(solution)/shard_map/all_gather | solution.py:157
  293.9 11.4 slice-start.4
  294.3 11.0 slice-start.5
  313.9 12.7 copy-start.3
  325.1 46.0 %collective-permute-start = (bf16[192,32,32]{0,2,1:T(8,128)(2,1)}, bf16[192,32,32]{0,2,1:T(8,128)(2,1)}, u32[]{:S(2)}, u32[]{:S(2)}) collective-permute-start(bf16[192,32,32]{0,2,1:T(8,128)(2,1)} %get-tuple-element.32), channel_id=1, source_target_pairs={{0,4},{4,8},{8,12},{12,16},{16,20},{20,24},{24,28},{28,0},{1,5},{5... | collective-permute-start | bytes 1179656 | tf_op jit(solution)/shard_map/ppermute | solution.py:32
  325.1 57.2 %collective-permute-start.1 = (bf16[192,32,32]{0,2,1:T(8,128)(2,1)}, bf16[192,32,32]{0,2,1:T(8,128)(2,1)}, u32[]{:S(2)}, u32[]{:S(2)}) collective-permute-start(bf16[192,32,32]{0,2,1:T(8,128)(2,1)} %get-tuple-element.31), channel_id=1, source_target_pairs={{0,8},{4,12},{8,16},{12,20},{16,24},{20,28},{24,0},{28,4},{1,9},{5... | collective-permute-start | bytes 1179656 | tf_op jit(solution)/shard_map/ppermute | solution.py:32
  326.6 151.6 %copy-start.30 = (s32[1024]{0:T(1024)}, s32[1024]{0:T(1024)S(1)}, u32[]{:S(2)}) copy-start(s32[1024]{0:T(1024)S(1)} %pad_clamp_fusion) | copy-start | bytes 12292
  332.8 113.7 %collective-permute-start.2 = (bf16[192,32,32]{0,2,1:T(8,128)(2,1)}, bf16[192,32,32]{0,2,1:T(8,128)(2,1)S(1)}, u32[]{:S(2)}, u32[]{:S(2)}) collective-permute-start(bf16[192,32,32]{0,2,1:T(8,128)(2,1)} %get-tuple-element.30), channel_id=1, source_target_pairs={{0,12},{4,16},{8,20},{12,24},{16,28},{20,0},{24,4},{28,8},{1,13},{... | collective-permute-start | bytes 1179656 | tf_op jit(solution)/shard_map/ppermute | solution.py:32
  334.0 140.9 %collective-permute-start.3 = (bf16[192,32,32]{0,2,1:T(8,128)(2,1)}, bf16[192,32,32]{0,2,1:T(8,128)(2,1)S(1)}, u32[]{:S(2)}, u32[]{:S(2)}) collective-permute-start(bf16[192,32,32]{0,2,1:T(8,128)(2,1)} %get-tuple-element.29), channel_id=1, source_target_pairs={{0,16},{4,20},{8,24},{12,28},{16,0},{20,4},{24,8},{28,12},{1,17},{... | collective-permute-start | bytes 1179656 | tf_op jit(solution)/shard_map/ppermute | solution.py:32
  335.2 140.5 %collective-permute-start.4 = (bf16[192,32,32]{0,2,1:T(8,128)(2,1)}, bf16[192,32,32]{0,2,1:T(8,128)(2,1)S(1)}, u32[]{:S(2)}, u32[]{:S(2)}) collective-permute-start(bf16[192,32,32]{0,2,1:T(8,128)(2,1)} %get-tuple-element.28), channel_id=1, source_target_pairs={{0,20},{4,24},{8,28},{12,0},{16,4},{20,8},{24,12},{28,16},{1,21},{... | collective-permute-start | bytes 1179656 | tf_op jit(solution)/shard_map/ppermute | solution.py:32
  371.0 105.5 %collective-permute-start.5 = (bf16[192,32,32]{0,2,1:T(8,128)(2,1)}, bf16[192,32,32]{0,2,1:T(8,128)(2,1)S(1)}, u32[]{:S(2)}, u32[]{:S(2)}) collective-permute-start(bf16[192,32,32]{0,2,1:T(8,128)(2,1)} %get-tuple-element.27), channel_id=1, source_target_pairs={{0,24},{4,28},{8,0},{12,4},{16,8},{20,12},{24,16},{28,20},{1,25},{... | collective-permute-start | bytes 1179656 | tf_op jit(solution)/shard_map/ppermute | solution.py:32
  382.3 95.1 %collective-permute-start.6 = (bf16[192,32,32]{0,2,1:T(8,128)(2,1)}, bf16[192,32,32]{0,2,1:T(8,128)(2,1)S(1)}, u32[]{:S(2)}, u32[]{:S(2)}) collective-permute-start(bf16[192,32,32]{0,2,1:T(8,128)(2,1)} %get-tuple-element.26), channel_id=1, source_target_pairs={{0,28},{4,0},{8,4},{12,8},{16,12},{20,16},{24,20},{28,24},{1,29},{... | collective-permute-start | bytes 1179656 | tf_op jit(solution)/shard_map/ppermute | solution.py:32
  490.8 88.7 %all-to-all-start.5 = ((bf16[192,32,256]{0,1,2:T(8,128)(2,1)}), bf16[192,32,256]{0,1,2:T(8,128)(2,1)}, u32[]{:S(2)}, u32[]{:S(2)}) async-start(bf16[192,32,256]{0,1,2:T(8,128)(2,1)} %copy.226), calls=%async_computation.5 | async-start | bytes 8388608 | tf_op jit(solution)/shard_map/all_to_all | solution.py:140
  517.1 7.2 copy-start.31
  521.2 9.6 collective-permute-start.8
  522.5 8.3 collective-permute-start.7
  524.3 48.8 %copy-start.12 = (f32[192,1]{0,1:T(1,128)}, f32[192,1]{0,1:T(1,128)S(1)}, u32[]{:S(2)}) copy-start(f32[192,1]{0,1:T(1,128)S(1)} %get-tuple-element.37) | copy-start | bytes 2308
  524.3 48.8 %copy-start.14 = (f32[192,1]{0,1:T(1,128)}, f32[192,1]{0,1:T(1,128)S(1)}, u32[]{:S(2)}) copy-start(f32[192,1]{0,1:T(1,128)S(1)} %get-tuple-element.38) | copy-start | bytes 2308
  524.3 48.8 %copy-start.16 = (f32[192,1]{0,1:T(1,128)}, f32[192,1]{0,1:T(1,128)S(1)}, u32[]{:S(2)}) copy-start(f32[192,1]{0,1:T(1,128)S(1)} %get-tuple-element.39) | copy-start | bytes 2308
  524.3 48.8 %copy-start.18 = (f32[192,1]{0,1:T(1,128)}, f32[192,1]{0,1:T(1,128)S(1)}, u32[]{:S(2)}) copy-start(f32[192,1]{0,1:T(1,128)S(1)} %get-tuple-element.40) | copy-start | bytes 2308
  524.3 48.8 %copy-start.20 = (f32[192,1]{0,1:T(1,128)}, f32[192,1]{0,1:T(1,128)S(1)}, u32[]{:S(2)}) copy-start(f32[192,1]{0,1:T(1,128)S(1)} %get-tuple-element.41) | copy-start | bytes 2308
  524.3 48.8 %copy-start.22 = (f32[192,1]{0,1:T(1,128)}, f32[192,1]{0,1:T(1,128)S(1)}, u32[]{:S(2)}) copy-start(f32[192,1]{0,1:T(1,128)S(1)} %get-tuple-element.42) | copy-start | bytes 2308
  524.3 48.8 %copy-start.24 = (f32[192,1]{0,1:T(1,128)}, f32[192,1]{0,1:T(1,128)S(1)}, u32[]{:S(2)}) copy-start(f32[192,1]{0,1:T(1,128)S(1)} %get-tuple-element.43) | copy-start | bytes 2308
  524.3 48.8 %copy-start.26 = (f32[192,1]{0,1:T(1,128)}, f32[192,1]{0,1:T(1,128)S(1)}, u32[]{:S(2)}) copy-start(f32[192,1]{0,1:T(1,128)S(1)} %get-tuple-element.44) | copy-start | bytes 2308
  524.3 48.8 %copy-start.28 = (f32[192,1]{0,1:T(1,128)}, f32[192,1]{0,1:T(1,128)S(1)}, u32[]{:S(2)}) copy-start(f32[192,1]{0,1:T(1,128)S(1)} %get-tuple-element.45) | copy-start | bytes 2308
  579.4 52.2 %all-to-all-start.3 = ((bf16[192,32,256]{0,1,2:T(8,128)(2,1)}), bf16[192,32,256]{0,1,2:T(8,128)(2,1)}, u32[]{:S(2)}, u32[]{:S(2)}) async-start(bf16[192,32,256]{0,1,2:T(8,128)(2,1)} %copy.218), calls=%async_computation.3 | async-start | bytes 8388608 | tf_op jit(solution)/shard_map/all_to_all | solution.py:140
  673.6 80.0 %copy-start.8 = (f32[768,32,64]{0,2,1:T(8,128)}, f32[768,32,64]{0,2,1:T(8,128)S(1)}, u32[]{:S(2)}) copy-start(f32[768,32,64]{0,2,1:T(8,128)S(1)} %subtract_multiply_fusion) | copy-start | bytes 18874372
  753.6 22.7 %copy-start.11 = (f32[32,64]{1,0:T(8,128)S(1)}, f32[32,64]{1,0:T(8,128)}, u32[]{:S(2)}) copy-start(f32[32,64]{1,0:T(8,128)} %copy-done.10) | copy-start | bytes 24580
  886.7 9.6 copy-start.4
  900.3 14.5 copy-start.13
  900.3 14.5 copy-start.15
  900.4 14.5 copy-start.17
  900.4 14.5 copy-start.19
  900.4 14.5 copy-start.21
  900.4 14.5 copy-start.23
  900.4 14.5 copy-start.25
  900.4 14.5 copy-start.27
  900.4 14.5 copy-start.29
  900.7 7.7 collective-permute-start.10
  904.8 7.5 collective-permute-start.9
  948.2 100.8 %all-to-all-start.8 = ((bf16[192,256,32]{0,2,1:T(8,128)(2,1)}), bf16[192,256,32]{0,2,1:T(8,128)(2,1)}, u32[]{:S(2)}, u32[]{:S(2)}) async-start(bf16[192,256,32]{0,2,1:T(8,128)(2,1)} %copy.240), calls=%async_computation.8 | async-start | bytes 8388608 | tf_op jit(solution)/shard_map/all_to_all | solution.py:76
  1049.0 97.5 %all-to-all-start.7 = ((bf16[192,256,32]{0,2,1:T(8,128)(2,1)}), bf16[192,256,32]{0,2,1:T(8,128)(2,1)}, u32[]{:S(2)}, u32[]{:S(2)}) async-start(bf16[192,256,32]{0,2,1:T(8,128)(2,1)} %copy.236), calls=%async_computation.7 | async-start | bytes 8388608 | tf_op jit(solution)/shard_map/all_to_all | solution.py:73
  1146.5 83.7 %all-to-all-start.4 = ((bf16[4,2,196608]{2,1,0:T(2,128)(2,1)}), bf16[4,2,196608]{2,1,0:T(2,128)(2,1)}, u32[]{:S(2)}, u32[]{:S(2)}) async-start(bf16[4,2,196608]{2,1,0:T(2,128)(2,1)} %reshape.210), calls=%async_computation.4 | async-start | bytes 6291456 | tf_op jit(solution)/shard_map/all_to_all | solution.py:144
  1164.7 8.2 copy-start.7
  1164.7 17.5 %slice-start = ((s8[6291456]{0:T(1024)(128)(4,1)}), s8[4194304]{0:T(1024)(128)(4,1)S(1)}, s32[]{:S(2)}) async-start(s8[6291456]{0:T(1024)(128)(4,1)} %bitcast.333), calls=%async_computation.12 | async-start | bytes 8388608
  1172.9 9.3 slice-start.1
  1205.3 11.1 copy-start.1
  1230.2 205.4 %all-to-all-start.9 = ((bf16[192,32,256]{0,1,2:T(8,128)(2,1)}), bf16[192,32,256]{0,1,2:T(8,128)(2,1)}, u32[]{:S(2)}, u32[]{:S(2)}) async-start(bf16[192,32,256]{0,1,2:T(8,128)(2,1)} %copy.245), calls=%async_computation.9 | async-start | bytes 8388608 | tf_op jit(solution)/shard_map/all_to_all | solution.py:89
  1267.6 27.7 %slice-start.6 = ((s8[6291456]{0:T(1024)(128)(4,1)}), s8[2097152]{0:T(1024)(128)(4,1)S(1)}, s32[]{:S(2)}) async-start(s8[6291456]{0:T(1024)(128)(4,1)} %bitcast.339), calls=%async_computation.18 | async-start | bytes 4194304
  1277.0 18.3 %slice-start.7 = ((s8[6291456]{0:T(1024)(128)(4,1)}), s8[4194304]{0:T(1024)(128)(4,1)S(1)}, s32[]{:S(2)}) async-start(s8[6291456]{0:T(1024)(128)(4,1)} %bitcast.339), calls=%async_computation.19 | async-start | bytes 8388608
  1313.6 19.1 %collective-permute-start.11 = (bf16[192,32,32]{0,2,1:T(8,128)(2,1)S(1)}, bf16[192,32,32]{0,2,1:T(8,128)(2,1)S(1)}, u32[]{:S(2)}, u32[]{:S(2)}) collective-permute-start(bf16[192,32,32]{0,2,1:T(8,128)(2,1)S(1)} %get-tuple-element.23), channel_id=1, source_target_pairs={{0,4},{4,8},{8,12},{12,16},{16,20},{20,24},{24,28},{28,0},{1,5},{5... | collective-permute-start | bytes 1179656 | tf_op jit(solution)/shard_map/ppermute | solution.py:32
  1313.7 35.3 %collective-permute-start.12 = (bf16[192,32,32]{0,2,1:T(8,128)(2,1)S(1)}, bf16[192,32,32]{0,2,1:T(8,128)(2,1)S(1)}, u32[]{:S(2)}, u32[]{:S(2)}) collective-permute-start(bf16[192,32,32]{0,2,1:T(8,128)(2,1)S(1)} %get-tuple-element.22), channel_id=1, source_target_pairs={{0,8},{4,12},{8,16},{12,20},{16,24},{20,28},{24,0},{28,4},{1,9},{5... | collective-permute-start | bytes 1179656 | tf_op jit(solution)/shard_map/ppermute | solution.py:32
  1315.1 72.9 %collective-permute-start.13 = (bf16[192,32,32]{0,2,1:T(8,128)(2,1)S(1)}, bf16[192,32,32]{0,2,1:T(8,128)(2,1)S(1)}, u32[]{:S(2)}, u32[]{:S(2)}) collective-permute-start(bf16[192,32,32]{0,2,1:T(8,128)(2,1)S(1)} %get-tuple-element.21), channel_id=1, source_target_pairs={{0,12},{4,16},{8,20},{12,24},{16,28},{20,0},{24,4},{28,8},{1,13},{... | collective-permute-start | bytes 1179656 | tf_op jit(solution)/shard_map/ppermute | solution.py:32
  1316.3 102.3 %collective-permute-start.14 = (bf16[192,32,32]{0,2,1:T(8,128)(2,1)S(1)}, bf16[192,32,32]{0,2,1:T(8,128)(2,1)S(1)}, u32[]{:S(2)}, u32[]{:S(2)}) collective-permute-start(bf16[192,32,32]{0,2,1:T(8,128)(2,1)S(1)} %get-tuple-element.20), channel_id=1, source_target_pairs={{0,16},{4,20},{8,24},{12,28},{16,0},{20,4},{24,8},{28,12},{1,17},{... | collective-permute-start | bytes 1179656 | tf_op jit(solution)/shard_map/ppermute | solution.py:32
  1317.5 101.9 %collective-permute-start.15 = (bf16[192,32,32]{0,2,1:T(8,128)(2,1)S(1)}, bf16[192,32,32]{0,2,1:T(8,128)(2,1)S(1)}, u32[]{:S(2)}, u32[]{:S(2)}) collective-permute-start(bf16[192,32,32]{0,2,1:T(8,128)(2,1)S(1)} %get-tuple-element.19), channel_id=1, source_target_pairs={{0,20},{4,24},{8,28},{12,0},{16,4},{20,8},{24,12},{28,16},{1,21},{... | collective-permute-start | bytes 1179656 | tf_op jit(solution)/shard_map/ppermute | solution.py:32
  1332.7 87.5 %collective-permute-start.16 = (bf16[192,32,32]{0,2,1:T(8,128)(2,1)S(1)}, bf16[192,32,32]{0,2,1:T(8,128)(2,1)S(1)}, u32[]{:S(2)}, u32[]{:S(2)}) collective-permute-start(bf16[192,32,32]{0,2,1:T(8,128)(2,1)S(1)} %get-tuple-element.18), channel_id=1, source_target_pairs={{0,24},{4,28},{8,0},{12,4},{16,8},{20,12},{24,16},{28,20},{1,25},{... | collective-permute-start | bytes 1179656 | tf_op jit(solution)/shard_map/ppermute | solution.py:32
  1349.0 72.1 %collective-permute-start.17 = (bf16[192,32,32]{0,2,1:T(8,128)(2,1)S(1)}, bf16[192,32,32]{0,2,1:T(8,128)(2,1)S(1)}, u32[]{:S(2)}, u32[]{:S(2)}) collective-permute-start(bf16[192,32,32]{0,2,1:T(8,128)(2,1)S(1)} %get-tuple-element.17), channel_id=1, source_target_pairs={{0,28},{4,0},{8,4},{12,8},{16,12},{20,16},{24,20},{28,24},{1,29},{... | collective-permute-start | bytes 1179656 | tf_op jit(solution)/shard_map/ppermute | solution.py:32
  1442.3 14.1 slice-start.2
  (8 other events, 33.4 us)
Sparse Core Ops, SparseCore 0:
  130.3 39.0 all-gather.2
  295.8 39.0 all-gather.4
